TPU v7x, 32 devices: a whole 2x2x4 slice. The times are simulated.
32 devices in a mesh: slab: 4 (over x, core), trace: 8 (over z, y).
Axes of the slice: x: 2, y: 2, z: 4, core: 2. Of those that a mesh axis runs over, the one named last changes fastest.
Arguments:
- incident: float32 [4, 3072, 128], P(None, 'trace'), may hold values from -6 to 6
- green_interior: bfloat16 [4, 2, 4608, 3072], P('slab', None, 'trace'), may hold values from -0.078125 to 0.078125
- green_next: bfloat16 [4, 2, 3072, 3072], P('slab', None, 'trace'), may hold values from -0.0625 to 0.0625
- sources: float32 [4, 4, 3072, 128], P('slab', None, 'trace'), may hold values from -3 to 3
Outputs:
- interior: float32 [4, 4, 4608, 128], P('slab', None, 'trace')
- traces: float32 [4, 4, 3072, 128], P('slab', None, 'trace')
All inputs are finite; a program needn't handle non-finite values.
Results may differ from a plain program's by a relative error of at most 0.014.
Values may be sent and summed in bfloat16 or wider, within the bound.
A program may use at most 64 MiB of HBM per device.

v0:
```python
import jax
import jax.numpy as jnp
from jax import lax
from jax.sharding import PartitionSpec as P


def shifted(value, axis, steps):
    count = lax.axis_size(axis)
    initial, last = (max(0, -steps), min(count, count - steps))
    return lax.ppermute(value, axis, [(source, source + steps) for source in range(initial, last)])


def complex_apply(halves, vectors, batches):
    row_count = halves.shape[1]
    inner_width = halves.shape[2]
    half_cols = vectors.shape[1] // (2 * batches)
    product = jnp.dot(
        halves.reshape(2 * row_count, inner_width), vectors, preferred_element_type=jnp.float32
    )
    product = product.reshape(2, row_count, batches, 2, half_cols)
    real_part = product[0, :, :, 0] - product[1, :, :, 1]
    imag_part = product[0, :, :, 1] + product[1, :, :, 0]
    return jnp.stack([real_part, imag_part], axis=2)


def to_fronts(product):
    row_count, batches, two_parts, half_cols = product.shape
    return jnp.transpose(product, (1, 0, 2, 3)).reshape(batches, row_count, two_parts * half_cols)


def local(incident, green_interior, green_next, sources):
    slab_count = lax.axis_size("slab")
    position = lax.axis_index("slab")
    fronts = incident.shape[0]
    local_rows = incident.shape[1]
    columns = incident.shape[2]
    total_steps = fronts + slab_count - 1
    next_halves = green_next[0]
    inner_halves = green_interior[0]
    local_sources = sources[0]

    def advance(counter, carried):
        received, leaving_all, inner_all, stored = carried
        front_index = counter - position
        active = (front_index >= 0) & (front_index < fronts)
        chosen = jnp.clip(front_index, 0, fronts - 1)
        start_front = jnp.clip(counter, 0, fronts - 1).astype(jnp.int32)
        boundary = lax.dynamic_index_in_dim(incident, start_front, 0, keepdims=False).astype(
            jnp.bfloat16
        )
        entering = jnp.where(position == 0, boundary, received)
        gathered = lax.all_gather(entering, "trace", axis=0, tiled=True)
        own_source = lax.dynamic_index_in_dim(local_sources, chosen, 0, keepdims=False)
        leaving = to_fronts(complex_apply(next_halves, gathered, 1))[0] + own_source
        previous = lax.dynamic_index_in_dim(leaving_all, chosen, 0, keepdims=False)
        leaving_all = lax.dynamic_update_index_in_dim(
            leaving_all, jnp.where(active, leaving, previous), chosen, 0
        )
        received = shifted(leaving.astype(jnp.bfloat16), "slab", 1)
        previous_cols = lax.dynamic_slice_in_dim(stored, chosen * columns, columns, 1)
        stored = lax.dynamic_update_slice_in_dim(
            stored, jnp.where(active, gathered, previous_cols), chosen * columns, 1
        )
        return (received, leaving_all, inner_all, stored)

    received_start = jnp.zeros((local_rows, columns), jnp.bfloat16)
    leaving_start = jnp.zeros((fronts, local_rows, columns), jnp.float32)
    inner_start = jnp.zeros((1, 1), jnp.float32)
    stored_start = jnp.zeros((next_halves.shape[2], fronts * columns), jnp.bfloat16)

    def step_without(counter, carried):
        return advance(counter, carried)

    final_state = lax.fori_loop(
        0, total_steps, step_without, (received_start, leaving_start, inner_start, stored_start)
    )
    interior_rows = to_fronts(complex_apply(inner_halves, final_state[3], fronts))
    return (interior_rows[None], final_state[1][None])


def solution(mesh):
    return jax.shard_map(
        local,
        mesh=mesh,
        in_specs=(
            P(None, "trace", None),
            P("slab", None, "trace", None),
            P("slab", None, "trace", None),
            P("slab", None, "trace", None),
        ),
        out_specs=(P("slab", None, "trace", None), P("slab", None, "trace", None)),
        check_vma=False,
    )
```

profile of v0, /device:TPU:23, one launch (start us, length us, event | category | flops | bytes accessed | tf_op | source)
XLA Modules:
  0.0 333.7 jit_solution(6273158393734383576)
XLA Ops:
  6.1 310.0 %while.18 = (s32[]{:T(128)}, bf16[384,128]{0,1:T(8,128)(2,1)S(1)}, f32[4,384,128]{2,1,0:T(8,128)S(1)}, bf16[3072,512]{0,1:T(8,128)(2,1)}, pred[]{:T(512)}, /*ind...) while((s32[]{:T(128)}, bf16[384,128]{0,1:T(8,128)(2,1)S(1)}, ...), condition=%wide.region_1.2_spmd, body=%wide.region_0.1_spmd.sunk | while | flops 604717056 | bytes 15434059 | solution.py:74
  7.2 24.4 %all_gather.9 = bf16[3072,128]{0,1:T(8,128)(2,1)S(1)} all-gather(bf16[384,128]{0,1:T(8,128)(2,1)S(1)} %bitcast_select_fusion.2), channel_id=1, replica_groups=mesh['slab'=4,'trace'=8] {'trace'}, dimensions={0}, use_global_device_ids=true | all-gather | bytes 884736 | tf_op jit(solution)/shard_map/while/body/eval_jaxpr/all_gather | solution.py:52
  31.6 4.0 %convolution_bitcast_fusion.3 = f32[768,128]{0,1:T(8,128)S(1)} fusion(bf16[3072,128]{0,1:T(8,128)(2,1)S(1)} %all_gather.9, bf16[768,3072]{1,0:T(8,128)(2,1)} %bitcast.73), kind=kOutput, calls=%fused_computation.clone.1 | convolution fusion | flops 603979776 | bytes 5898240 | tf_op jit(solution)/shard_map/while/body/eval_jaxpr/dot_general | solution.py:17
  40.8 6.0 %collective-permute-done = bf16[384,128]{0,1:T(8,128)(2,1)S(1)} collective-permute-done((bf16[384,128]{0,1:T(8,128)(2,1)S(1)}, bf16[384,128]{0,1:T(8,128)(2,1)S(1)}, u32[]{:S(2)}, u32[]{:S(2)}) %collective-permute-start) | collective-permute-done | bytes 98336 | tf_op jit(solution)/shard_map/while/body/eval_jaxpr/ppermute | solution.py:10
  47.9 27.8 %all_gather.9 = bf16[3072,128]{0,1:T(8,128)(2,1)S(1)} all-gather(bf16[384,128]{0,1:T(8,128)(2,1)S(1)} %bitcast_select_fusion.2), channel_id=1, replica_groups=mesh['slab'=4,'trace'=8] {'trace'}, dimensions={0}, use_global_device_ids=true | all-gather | bytes 884736 | tf_op jit(solution)/shard_map/while/body/eval_jaxpr/all_gather | solution.py:52
  75.7 4.0 %convolution_bitcast_fusion.3 = f32[768,128]{0,1:T(8,128)S(1)} fusion(bf16[3072,128]{0,1:T(8,128)(2,1)S(1)} %all_gather.9, bf16[768,3072]{1,0:T(8,128)(2,1)} %bitcast.73), kind=kOutput, calls=%fused_computation.clone.1 | convolution fusion | flops 603979776 | bytes 5898240 | tf_op jit(solution)/shard_map/while/body/eval_jaxpr/dot_general | solution.py:17
  84.8 6.9 %collective-permute-done = bf16[384,128]{0,1:T(8,128)(2,1)S(1)} collective-permute-done((bf16[384,128]{0,1:T(8,128)(2,1)S(1)}, bf16[384,128]{0,1:T(8,128)(2,1)S(1)}, u32[]{:S(2)}, u32[]{:S(2)}) %collective-permute-start) | collective-permute-done | bytes 98336 | tf_op jit(solution)/shard_map/while/body/eval_jaxpr/ppermute | solution.py:10
  92.8 27.6 %all_gather.9 = bf16[3072,128]{0,1:T(8,128)(2,1)S(1)} all-gather(bf16[384,128]{0,1:T(8,128)(2,1)S(1)} %bitcast_select_fusion.2), channel_id=1, replica_groups=mesh['slab'=4,'trace'=8] {'trace'}, dimensions={0}, use_global_device_ids=true | all-gather | bytes 884736 | tf_op jit(solution)/shard_map/while/body/eval_jaxpr/all_gather | solution.py:52
  120.5 4.0 %convolution_bitcast_fusion.3 = f32[768,128]{0,1:T(8,128)S(1)} fusion(bf16[3072,128]{0,1:T(8,128)(2,1)S(1)} %all_gather.9, bf16[768,3072]{1,0:T(8,128)(2,1)} %bitcast.73), kind=kOutput, calls=%fused_computation.clone.1 | convolution fusion | flops 603979776 | bytes 5898240 | tf_op jit(solution)/shard_map/while/body/eval_jaxpr/dot_general | solution.py:17
  129.7 7.3 %collective-permute-done = bf16[384,128]{0,1:T(8,128)(2,1)S(1)} collective-permute-done((bf16[384,128]{0,1:T(8,128)(2,1)S(1)}, bf16[384,128]{0,1:T(8,128)(2,1)S(1)}, u32[]{:S(2)}, u32[]{:S(2)}) %collective-permute-start) | collective-permute-done | bytes 98336 | tf_op jit(solution)/shard_map/while/body/eval_jaxpr/ppermute | solution.py:10
  138.0 26.9 %all_gather.9 = bf16[3072,128]{0,1:T(8,128)(2,1)S(1)} all-gather(bf16[384,128]{0,1:T(8,128)(2,1)S(1)} %bitcast_select_fusion.2), channel_id=1, replica_groups=mesh['slab'=4,'trace'=8] {'trace'}, dimensions={0}, use_global_device_ids=true | all-gather | bytes 884736 | tf_op jit(solution)/shard_map/while/body/eval_jaxpr/all_gather | solution.py:52
  164.8 4.0 %convolution_bitcast_fusion.3 = f32[768,128]{0,1:T(8,128)S(1)} fusion(bf16[3072,128]{0,1:T(8,128)(2,1)S(1)} %all_gather.9, bf16[768,3072]{1,0:T(8,128)(2,1)} %bitcast.73), kind=kOutput, calls=%fused_computation.clone.1 | convolution fusion | flops 603979776 | bytes 5898240 | tf_op jit(solution)/shard_map/while/body/eval_jaxpr/dot_general | solution.py:17
  174.0 7.5 %collective-permute-done = bf16[384,128]{0,1:T(8,128)(2,1)S(1)} collective-permute-done((bf16[384,128]{0,1:T(8,128)(2,1)S(1)}, bf16[384,128]{0,1:T(8,128)(2,1)S(1)}, u32[]{:S(2)}, u32[]{:S(2)}) %collective-permute-start) | collective-permute-done | bytes 98336 | tf_op jit(solution)/shard_map/while/body/eval_jaxpr/ppermute | solution.py:10
  182.6 27.6 %all_gather.9 = bf16[3072,128]{0,1:T(8,128)(2,1)S(1)} all-gather(bf16[384,128]{0,1:T(8,128)(2,1)S(1)} %bitcast_select_fusion.2), channel_id=1, replica_groups=mesh['slab'=4,'trace'=8] {'trace'}, dimensions={0}, use_global_device_ids=true | all-gather | bytes 884736 | tf_op jit(solution)/shard_map/while/body/eval_jaxpr/all_gather | solution.py:52
  210.1 4.0 %convolution_bitcast_fusion.3 = f32[768,128]{0,1:T(8,128)S(1)} fusion(bf16[3072,128]{0,1:T(8,128)(2,1)S(1)} %all_gather.9, bf16[768,3072]{1,0:T(8,128)(2,1)} %bitcast.73), kind=kOutput, calls=%fused_computation.clone.1 | convolution fusion | flops 603979776 | bytes 5898240 | tf_op jit(solution)/shard_map/while/body/eval_jaxpr/dot_general | solution.py:17
  219.3 7.3 %collective-permute-done = bf16[384,128]{0,1:T(8,128)(2,1)S(1)} collective-permute-done((bf16[384,128]{0,1:T(8,128)(2,1)S(1)}, bf16[384,128]{0,1:T(8,128)(2,1)S(1)}, u32[]{:S(2)}, u32[]{:S(2)}) %collective-permute-start) | collective-permute-done | bytes 98336 | tf_op jit(solution)/shard_map/while/body/eval_jaxpr/ppermute | solution.py:10
  227.6 26.7 %all_gather.9 = bf16[3072,128]{0,1:T(8,128)(2,1)S(1)} all-gather(bf16[384,128]{0,1:T(8,128)(2,1)S(1)} %bitcast_select_fusion.2), channel_id=1, replica_groups=mesh['slab'=4,'trace'=8] {'trace'}, dimensions={0}, use_global_device_ids=true | all-gather | bytes 884736 | tf_op jit(solution)/shard_map/while/body/eval_jaxpr/all_gather | solution.py:52
  254.4 4.0 %convolution_bitcast_fusion.3 = f32[768,128]{0,1:T(8,128)S(1)} fusion(bf16[3072,128]{0,1:T(8,128)(2,1)S(1)} %all_gather.9, bf16[768,3072]{1,0:T(8,128)(2,1)} %bitcast.73), kind=kOutput, calls=%fused_computation.clone.1 | convolution fusion | flops 603979776 | bytes 5898240 | tf_op jit(solution)/shard_map/while/body/eval_jaxpr/dot_general | solution.py:17
  263.6 7.6 %collective-permute-done = bf16[384,128]{0,1:T(8,128)(2,1)S(1)} collective-permute-done((bf16[384,128]{0,1:T(8,128)(2,1)S(1)}, bf16[384,128]{0,1:T(8,128)(2,1)S(1)}, u32[]{:S(2)}, u32[]{:S(2)}) %collective-permute-start) | collective-permute-done | bytes 98336 | tf_op jit(solution)/shard_map/while/body/eval_jaxpr/ppermute | solution.py:10
  272.2 27.9 %all_gather.9 = bf16[3072,128]{0,1:T(8,128)(2,1)S(1)} all-gather(bf16[384,128]{0,1:T(8,128)(2,1)S(1)} %bitcast_select_fusion.2), channel_id=1, replica_groups=mesh['slab'=4,'trace'=8] {'trace'}, dimensions={0}, use_global_device_ids=true | all-gather | bytes 884736 | tf_op jit(solution)/shard_map/while/body/eval_jaxpr/all_gather | solution.py:52
  300.0 4.0 %convolution_bitcast_fusion.3 = f32[768,128]{0,1:T(8,128)S(1)} fusion(bf16[3072,128]{0,1:T(8,128)(2,1)S(1)} %all_gather.9, bf16[768,3072]{1,0:T(8,128)(2,1)} %bitcast.73), kind=kOutput, calls=%fused_computation.clone.1 | convolution fusion | flops 603979776 | bytes 5898240 | tf_op jit(solution)/shard_map/while/body/eval_jaxpr/dot_general | solution.py:17
  309.2 6.9 %collective-permute-done = bf16[384,128]{0,1:T(8,128)(2,1)S(1)} collective-permute-done((bf16[384,128]{0,1:T(8,128)(2,1)S(1)}, bf16[384,128]{0,1:T(8,128)(2,1)S(1)}, u32[]{:S(2)}, u32[]{:S(2)}) %collective-permute-start) | collective-permute-done | bytes 98336 | tf_op jit(solution)/shard_map/while/body/eval_jaxpr/ppermute | solution.py:10
  317.0 9.7 %convolution_bitcast_fusion.1 = f32[1152,512]{0,1:T(8,128)} fusion(bf16[3072,512]{0,1:T(8,128)(2,1)} %get-tuple-element.179, bf16[1152,3072]{1,0:T(8,128)(2,1)} %bitcast.77), kind=kOutput, calls=%fused_computation.18 | convolution fusion | flops 3623878656 | bytes 12582912 | tf_op jit(solution)/shard_map/dot_general | solution.py:17
  326.7 3.4 %reshape.114 = f32[2,576,4,2,64]{1,0,4,3,2:T(2,128)S(1)} reshape(f32[1152,512]{0,1:T(8,128)} %convolution_bitcast_fusion.1) | data formatting | bytes 4718592 | tf_op jit(solution)/shard_map/reshape | solution.py:20
  (123 shorter events, 52.6 us)
Async XLA Ops:
  37.1 9.7 %collective-permute-start = (bf16[384,128]{0,1:T(8,128)(2,1)S(1)}, bf16[384,128]{0,1:T(8,128)(2,1)S(1)}, u32[]{:S(2)}, u32[]{:S(2)}) collective-permute-start(bf16[384,128]{0,1:T(8,128)(2,1)S(1)} %fusion.20), channel_id=1, source_target_pairs={{0,8},{8,16},{16,24},{1,9},{9,17},{17,25},{2,10},{10,18},{18,26},{... | collective-permute-start | bytes 294920 | tf_op jit(solution)/shard_map/while/body/eval_jaxpr/ppermute | solution.py:10
  81.1 10.6 %collective-permute-start = (bf16[384,128]{0,1:T(8,128)(2,1)S(1)}, bf16[384,128]{0,1:T(8,128)(2,1)S(1)}, u32[]{:S(2)}, u32[]{:S(2)}) collective-permute-start(bf16[384,128]{0,1:T(8,128)(2,1)S(1)} %fusion.20), channel_id=1, source_target_pairs={{0,8},{8,16},{16,24},{1,9},{9,17},{17,25},{2,10},{10,18},{18,26},{... | collective-permute-start | bytes 294920 | tf_op jit(solution)/shard_map/while/body/eval_jaxpr/ppermute | solution.py:10
  125.9 11.0 %collective-permute-start = (bf16[384,128]{0,1:T(8,128)(2,1)S(1)}, bf16[384,128]{0,1:T(8,128)(2,1)S(1)}, u32[]{:S(2)}, u32[]{:S(2)}) collective-permute-start(bf16[384,128]{0,1:T(8,128)(2,1)S(1)} %fusion.20), channel_id=1, source_target_pairs={{0,8},{8,16},{16,24},{1,9},{9,17},{17,25},{2,10},{10,18},{18,26},{... | collective-permute-start | bytes 294920 | tf_op jit(solution)/shard_map/while/body/eval_jaxpr/ppermute | solution.py:10
  170.3 11.2 %collective-permute-start = (bf16[384,128]{0,1:T(8,128)(2,1)S(1)}, bf16[384,128]{0,1:T(8,128)(2,1)S(1)}, u32[]{:S(2)}, u32[]{:S(2)}) collective-permute-start(bf16[384,128]{0,1:T(8,128)(2,1)S(1)} %fusion.20), channel_id=1, source_target_pairs={{0,8},{8,16},{16,24},{1,9},{9,17},{17,25},{2,10},{10,18},{18,26},{... | collective-permute-start | bytes 294920 | tf_op jit(solution)/shard_map/while/body/eval_jaxpr/ppermute | solution.py:10
  215.6 11.0 %collective-permute-start = (bf16[384,128]{0,1:T(8,128)(2,1)S(1)}, bf16[384,128]{0,1:T(8,128)(2,1)S(1)}, u32[]{:S(2)}, u32[]{:S(2)}) collective-permute-start(bf16[384,128]{0,1:T(8,128)(2,1)S(1)} %fusion.20), channel_id=1, source_target_pairs={{0,8},{8,16},{16,24},{1,9},{9,17},{17,25},{2,10},{10,18},{18,26},{... | collective-permute-start | bytes 294920 | tf_op jit(solution)/shard_map/while/body/eval_jaxpr/ppermute | solution.py:10
  259.9 11.3 %collective-permute-start = (bf16[384,128]{0,1:T(8,128)(2,1)S(1)}, bf16[384,128]{0,1:T(8,128)(2,1)S(1)}, u32[]{:S(2)}, u32[]{:S(2)}) collective-permute-start(bf16[384,128]{0,1:T(8,128)(2,1)S(1)} %fusion.20), channel_id=1, source_target_pairs={{0,8},{8,16},{16,24},{1,9},{9,17},{17,25},{2,10},{10,18},{18,26},{... | collective-permute-start | bytes 294920 | tf_op jit(solution)/shard_map/while/body/eval_jaxpr/ppermute | solution.py:10
  305.5 10.6 %collective-permute-start = (bf16[384,128]{0,1:T(8,128)(2,1)S(1)}, bf16[384,128]{0,1:T(8,128)(2,1)S(1)}, u32[]{:S(2)}, u32[]{:S(2)}) collective-permute-start(bf16[384,128]{0,1:T(8,128)(2,1)S(1)} %fusion.20), channel_id=1, source_target_pairs={{0,8},{8,16},{16,24},{1,9},{9,17},{17,25},{2,10},{10,18},{18,26},{... | collective-permute-start | bytes 294920 | tf_op jit(solution)/shard_map/while/body/eval_jaxpr/ppermute | solution.py:10
  316.2 0.9 copy-start
where the time goes:
time: 340 us; the launch traced here: 334 us
  blocking collectives  189 us (56%)
  waiting for transfers between devices  49.4 us (15%)
  matrix products  37.8 us (11%)
  other arithmetic  24.6 us (7%)
  local copies, waits for them, and re-layouts  22.4 us (7%)
  starting transfers between devices  9.04 us (3%)
    all_gather x7, blocking collectives, advance(): gathered = lax.all_gather(entering, 'trace', axis=0, tiled=True)  189 us
    ppermute x7, waiting for transfers between devices, shifted(): lax.ppermute(value, axis, [(source, source + steps) for source in range(i...  49.4 us
    dot_general x8, matrix products, complex_apply(): jnp.dot(halves.reshape(2 * row_count, inner_width), vectors, preferred_el...  37.8 us
    dynamic_update_slice x7, other arithmetic, advance(): lax.dynamic_update_slice_in_dim(stored, jnp.where(active, gathered, previ...  15.5 us
    ppermute x7, starting transfers between devices, shifted(): lax.ppermute(value, axis, [(source, source + steps) for source in range(i...  9.04 us
    dynamic_slice x14, local copies, waits for them, and re-layouts, advance(): lax.dynamic_index_in_dim(incident, start_front, 0, keepdims=False)  7.15 us
  transfers between devices with their start and end apart: 7, of which 7 were waited for; matrix products, arithmetic and copies ran while one was open for 5% of the time, Pallas kernels for 0%

commit v1 on v0

v1 whole, which is shorter than its diff:
```python
import functools

import jax
import jax.numpy as jnp
from jax import lax
from jax.experimental import pallas as pl
from jax.experimental.pallas import tpu as pltpu
from jax.sharding import PartitionSpec as P

MESH = pl.DeviceIdType.MESH
INNER = 2


def chunk_count(blocks, rows):
    count = 4
    while count > 1 and (blocks % (count * INNER) or (blocks // count * rows) % 128):
        count //= 2
    return count


def combine(first, second):
    lane = lax.broadcasted_iota(jnp.int32, first.shape, 1)
    half = first.shape[1] // 2
    turned = pltpu.roll(second, half, 1)
    return first + jnp.where(lane < half, -turned, turned)


def kernel(
    slabs,
    blocks,
    incident,
    green_interior,
    green_next,
    sources,
    interior,
    traces,
    entering,
    leaving,
    next_op,
    inner_op,
    incoming,
    own_sources,
    next_sum,
    inner_sum,
    trace_out,
    inner_out,
    recv_sem,
    direct_sem,
    relay_sem,
    load_sem,
    store_sem,
):
    fronts, _, rows, columns = entering.shape
    inner_rows = inner_op.shape[1]
    depth = next_op.shape[2]
    outer = blocks // INNER
    chunks = chunk_count(blocks, rows)
    per_chunk = blocks // chunks
    width = depth // chunks
    slab = lax.axis_index("slab")
    me = lax.axis_index("trace")
    lane_pos = lax.rem(me, INNER)
    my_outer = me // INNER
    partner = me + 1 - 2 * lane_pos
    first_slab = slab == 0
    last_slab = slab == slabs - 1
    my_chunk = me // per_chunk

    load_incident = pltpu.make_async_copy(incident, incoming, load_sem.at[0])
    load_next = pltpu.make_async_copy(green_next.at[0], next_op, load_sem.at[1])
    load_sources = pltpu.make_async_copy(sources.at[0], own_sources, load_sem.at[2])
    load_inner = pltpu.make_async_copy(green_interior.at[0], inner_op, load_sem.at[3])

    @pl.when(first_slab)
    def _():
        load_incident.start()

    load_next.start()
    load_sources.start()
    load_inner.start()

    barrier = pltpu.get_barrier_semaphore()

    def greet(target_slab, target):
        pl.semaphore_signal(
            barrier, inc=1, device_id={"slab": target_slab, "trace": target}, device_id_type=MESH
        )

    greet(slab, partner)

    @pl.when(first_slab)
    def _():
        for step in range(1, outer):
            greet(slab, lax.rem(my_outer + step, outer) * INNER + lane_pos)

    @pl.when(jnp.logical_not(first_slab))
    def _():
        for step in range(outer):
            greet(slab - 1, lax.rem(my_outer + step, outer) * INNER + lane_pos)

    peers = jnp.where(first_slab, outer, 1) + jnp.where(last_slab, 0, outer)
    pl.semaphore_wait(barrier, peers)

    def first_copy(front, step):
        target = lax.rem(my_outer + step, outer) * INNER + lane_pos
        return pltpu.make_async_remote_copy(
            src_ref=entering.at[front, me],
            dst_ref=entering.at[front, me],
            send_sem=direct_sem.at[1, front, step],
            recv_sem=recv_sem.at[front, me],
            device_id={"slab": slab, "trace": target},
            device_id_type=MESH,
        )

    def next_copy(front, step):
        target = lax.rem(my_outer + step, outer) * INNER + lane_pos
        return pltpu.make_async_remote_copy(
            src_ref=leaving.at[front],
            dst_ref=entering.at[front, me],
            send_sem=direct_sem.at[0, front, step],
            recv_sem=recv_sem.at[front, me],
            device_id={"slab": slab + 1, "trace": target},
            device_id_type=MESH,
        )

    def relay_copy(front, block):
        return pltpu.make_async_remote_copy(
            src_ref=entering.at[front, block],
            dst_ref=entering.at[front, block],
            send_sem=relay_sem.at[front, block // INNER],
            recv_sem=recv_sem.at[front, block],
            device_id={"slab": slab, "trace": partner},
            device_id_type=MESH,
        )

    def store_trace(front):
        return pltpu.make_async_copy(
            trace_out.at[front], traces.at[0, front], store_sem.at[0, front]
        )

    def store_inner(front):
        return pltpu.make_async_copy(
            inner_out.at[front], interior.at[0, front], store_sem.at[1, front]
        )

    @pl.when(first_slab)
    def _():
        load_incident.wait()
        for front in range(fronts):
            entering[front, me] = incoming[front].astype(jnp.bfloat16)
        for step in range(1, outer):
            first_copy(0, step).start()

    def chunk_at(order):
        return lax.rem(my_chunk + order, chunks)

    def vectors(front, chunk):
        return entering[front, pl.ds(chunk * per_chunk, per_chunk)].reshape(width, columns)

    def add_chunk(op, total, front, chunk, fresh):
        start = pl.multiple_of(chunk * width, width)
        halves = op.shape[1]
        matrix = op[:, :, pl.ds(start, width)].reshape(2 * halves, width)
        product = jnp.dot(
            matrix, vectors(front, chunk), preferred_element_type=jnp.float32
        )
        if fresh:
            total[...] = product
        else:
            total[...] += product

    def inner_chunk(front, order):
        add_chunk(inner_op, inner_sum, front, chunk_at(order), order == 0)
        if order == chunks - 1:
            inner_out[front] = combine(inner_sum[0:inner_rows], inner_sum[inner_rows:])
            store_inner(front).start()

    def one_front(front, carry):
        @pl.when(first_slab & (front + 1 < fronts))
        def _():
            for step in range(1, outer):
                first_copy(front + 1, step).start()

        for order in range(chunks):
            for index in range(per_chunk // INNER):
                block = chunk_at(order) * per_chunk + index * INNER + lane_pos

                @pl.when(jnp.logical_not(first_slab & (block == me)))
                def _():
                    relay_copy(front, block).wait_recv()

                relay_copy(front, block).start()

            @pl.when(front > 0)
            def _():
                inner_chunk(front - 1, order)

        @pl.when(front == 0)
        def _():
            load_next.wait()
            load_sources.wait()
            load_inner.wait()

        for order in range(chunks):
            for index in range(per_chunk // INNER):
                block = chunk_at(order) * per_chunk + index * INNER + 1 - lane_pos
                relay_copy(front, block).wait_recv()
            add_chunk(next_op, next_sum, front, chunk_at(order), order == 0)

        result = combine(next_sum[0:rows], next_sum[rows:]) + own_sources[front]
        trace_out[front] = result
        leaving[front] = result.astype(jnp.bfloat16)

        @pl.when(jnp.logical_not(last_slab))
        def _():
            for step in range(outer):
                next_copy(front, step).start()

        store_trace(front).start()
        return carry

    lax.fori_loop(0, fronts, one_front, 0)
    for order in range(chunks):
        inner_chunk(fronts - 1, order)

    def drain(front, carry):
        @pl.when(first_slab)
        def _():
            for step in range(1, outer):
                first_copy(front, step).wait_send()

        @pl.when(jnp.logical_not(last_slab))
        def _():
            for step in range(outer):
                next_copy(front, step).wait_send()

        for index in range(outer):
            relay_copy(front, index * INNER + lane_pos).wait_send()
        store_trace(front).wait()
        store_inner(front).wait()
        return carry

    lax.fori_loop(0, fronts, drain, 0)


def local(slabs, blocks, incident, green_interior, green_next, sources):
    fronts, rows, columns = incident.shape
    inner_rows = green_interior.shape[2]
    depth = green_next.shape[3]
    outer = blocks // INNER
    anywhere = pl.BlockSpec(memory_space=pl.ANY)
    return pl.pallas_call(
        functools.partial(kernel, slabs, blocks),
        out_shape=(
            jax.ShapeDtypeStruct((1, fronts, inner_rows, columns), jnp.float32),
            jax.ShapeDtypeStruct((1, fronts, rows, columns), jnp.float32),
        ),
        in_specs=[anywhere] * 4,
        out_specs=(anywhere, anywhere),
        scratch_shapes=[
            pltpu.VMEM((fronts, blocks, rows, columns), jnp.bfloat16),
            pltpu.VMEM((fronts, rows, columns), jnp.bfloat16),
            pltpu.VMEM((2, rows, depth), jnp.bfloat16),
            pltpu.VMEM((2, inner_rows, depth), jnp.bfloat16),
            pltpu.VMEM((fronts, rows, columns), jnp.float32),
            pltpu.VMEM((fronts, rows, columns), jnp.float32),
            pltpu.VMEM((2 * rows, columns), jnp.float32),
            pltpu.VMEM((2 * inner_rows, columns), jnp.float32),
            pltpu.VMEM((fronts, rows, columns), jnp.float32),
            pltpu.VMEM((fronts, inner_rows, columns), jnp.float32),
            pltpu.SemaphoreType.DMA((fronts, blocks)),
            pltpu.SemaphoreType.DMA((2, fronts, outer)),
            pltpu.SemaphoreType.DMA((fronts, outer)),
            pltpu.SemaphoreType.DMA((4,)),
            pltpu.SemaphoreType.DMA((2, fronts)),
        ],
        compiler_params=pltpu.CompilerParams(
            collective_id=0, has_side_effects=True, vmem_limit_bytes=48 * 1024 * 1024
        ),
    )(incident, green_interior, green_next, sources)


def solution(mesh):
    return jax.shard_map(
        functools.partial(local, mesh.shape["slab"], mesh.shape["trace"]),
        mesh=mesh,
        in_specs=(
            P(None, "trace", None),
            P("slab", None, "trace", None),
            P("slab", None, "trace", None),
            P("slab", None, "trace", None),
        ),
        out_specs=(P("slab", None, "trace", None), P("slab", None, "trace", None)),
        check_vma=False,
    )
```

time: 340 us -> 102 us (0.30); the launches traced: 334 us -> 102 us
  blocking collectives: 189 us -> 0 us
  Pallas kernels: 0 us -> 97.4 us
  waiting for transfers between devices: 49.4 us -> 0 us
  matrix products: 37.8 us -> 0 us
  other arithmetic: 24.6 us -> 0 us
  local copies, waits for them, and re-layouts: 22.4 us -> 4.15 us
  starting transfers between devices: 9.04 us -> 0 us
    all_gather x7 -> x0, blocking collectives: 189 us -> none  [advance(): gathered = lax.all_gather(entering, 'trace', axis=0, tiled=True)]
    pallas_call x0 -> x1, Pallas kernels: none -> 97.4 us  [local(): pl.pallas_call(functools.partial(kernel, slabs, blocks), out_shape=(jax.S...]
    ppermute x7 -> x0, waiting for transfers between devices: 49.4 us -> none  [shifted(): lax.ppermute(value, axis, [(source, source + steps) for source in range(i...]
    dot_general x8 -> x0, matrix products: 37.8 us -> none  [complex_apply(): jnp.dot(halves.reshape(2 * row_count, inner_width), vectors, preferred_el...]
    dynamic_update_slice x7 -> x0, other arithmetic: 15.5 us -> none  [advance(): lax.dynamic_update_slice_in_dim(stored, jnp.where(active, gathered, previ...]
    ppermute x7 -> x0, starting transfers between devices: 9.04 us -> none  [shifted(): lax.ppermute(value, axis, [(source, source + steps) for source in range(i...]
    dynamic_slice x28 -> x0, local copies, waits for them, and re-layouts: 8.42 us -> none  [the longest x14 7.15 us: advance(): lax.dynamic_index_in_dim(incident, start_front, 0, keepdims=False)]
    reshape x8 -> x0, local copies, waits for them, and re-layouts: 4.88 us -> none  [complex_apply(): product = product.reshape(2, row_count, batches, 2, half_cols)]
  transfers between devices with their start and end apart: 7 -> 0, of which waited for: 7 -> 0; matrix products, arithmetic and copies ran while one was open for 5% -> 0% of each run, Pallas kernels for 0% -> 0%
where the time goes in v1:
time: 102 us
  Pallas kernels  97.4 us (95%)
  local copies, waits for them, and re-layouts  4.15 us (4%)
    pallas_call x1, Pallas kernels, local(): pl.pallas_call(functools.partial(kernel, slabs, blocks), out_shape=(jax.S...  97.4 us
    unnamed x6, local copies, waits for them, and re-layouts  4.15 us

profile of v1, /device:TPU:23, one launch (start us, length us, event | category | flops | bytes accessed | tf_op | source)
XLA Modules:
  0.0 102.2 jit_solution(14671297378634445286)
XLA Ops:
  0.6 0.0 copy-start
  0.6 1.1 %copy-done = f32[4,384,128]{2,1,0:T(8,128)S(1)} copy-done((f32[4,384,128]{2,1,0:T(8,128)S(1)}, f32[4,384,128]{2,1,0:T(8,128)}, u32[]{:S(2)}) %copy-start) | copy-done | bytes 786456
  1.8 0.0 copy-start.1
  1.8 1.1 %copy-done.1 = f32[1,4,384,128]{3,2,1,0:T(8,128)S(1)} copy-done((f32[1,4,384,128]{3,2,1,0:T(8,128)S(1)}, f32[1,4,384,128]{3,2,1,0:T(8,128)}, u32[]{:S(2)}) %copy-start.1) | copy-done | bytes 786456
  2.9 97.4 %shard_map.59 = (f32[1,4,576,128]{3,2,1,0:T(8,128)S(1)}, f32[1,4,384,128]{3,2,1,0:T(8,128)S(1)}) custom-call(f32[4,384,128]{2,1,0:T(8,128)S(1)} %copy-done, bf16[1,2,576,3072]{3,2,1,0:T(8,128)(2,1)} %green_interior.1, bf16[1,2,384,3072]{3,2,1,0:T(8,128)(2,1)} %green_next.1, f32[1,4,384,128]{3,2,1,0:T(8,128)S(1)} %copy-done.1), custom_call_target="tpu_custom_call" | custom-call | tf_op jit(solution)/shard_map/pallas_call | solution.py:252
  100.3 1.0 copy.8
  101.3 0.9 copy.9
Async XLA Ops:
  0.6 1.1 %copy-start = (f32[4,384,128]{2,1,0:T(8,128)S(1)}, f32[4,384,128]{2,1,0:T(8,128)}, u32[]{:S(2)}) copy-start(f32[4,384,128]{2,1,0:T(8,128)} %incident.1) | copy-start | bytes 2359300
  1.8 1.1 %copy-start.1 = (f32[1,4,384,128]{3,2,1,0:T(8,128)S(1)}, f32[1,4,384,128]{3,2,1,0:T(8,128)}, u32[]{:S(2)}) copy-start(f32[1,4,384,128]{3,2,1,0:T(8,128)} %sources.1) | copy-start | bytes 2359300

commit v2 on v1

--- a/solution.py
+++ b/solution.py
@@ -16,6 +16,20 @@
     while count > 1 and (blocks % (count * INNER) or (blocks // count * rows) % 128):
         count //= 2
     return count
+
+
+def flip(value, mask):
+    result = value
+    bit = 1
+    while bit <= mask:
+        if mask & bit:
+            result = result + bit - 2 * bit * lax.rem(result // bit, 2)
+        bit *= 2
+    return result
+
+
+def visit_order(count):
+    return [0] + list(range(count - 1, 0, -1))
 
 
 def combine(first, second):
@@ -36,6 +50,7 @@
     traces,
     entering,
     leaving,
+    first_out,
     next_op,
     inner_op,
     incoming,
@@ -66,14 +81,19 @@
     last_slab = slab == slabs - 1
     my_chunk = me // per_chunk
 
-    load_incident = pltpu.make_async_copy(incident, incoming, load_sem.at[0])
-    load_next = pltpu.make_async_copy(green_next.at[0], next_op, load_sem.at[1])
-    load_sources = pltpu.make_async_copy(sources.at[0], own_sources, load_sem.at[2])
-    load_inner = pltpu.make_async_copy(green_interior.at[0], inner_op, load_sem.at[3])
-
-    @pl.when(first_slab)
-    def _():
-        load_incident.start()
+    def load_incident(front):
+        return pltpu.make_async_copy(
+            incident.at[front], incoming.at[front], load_sem.at[3 + front]
+        )
+
+    load_next = pltpu.make_async_copy(green_next.at[0], next_op, load_sem.at[0])
+    load_sources = pltpu.make_async_copy(sources.at[0], own_sources, load_sem.at[1])
+    load_inner = pltpu.make_async_copy(green_interior.at[0], inner_op, load_sem.at[2])
+
+    @pl.when(first_slab | last_slab)
+    def _():
+        for front in range(fronts):
+            load_incident(front).start()
 
     load_next.start()
     load_sources.start()
@@ -86,40 +106,41 @@
             barrier, inc=1, device_id={"slab": target_slab, "trace": target}, device_id_type=MESH
         )
 
+    def row_peer(step):
+        return flip(my_outer, step) * INNER + lane_pos
+
     greet(slab, partner)
 
     @pl.when(first_slab)
     def _():
         for step in range(1, outer):
-            greet(slab, lax.rem(my_outer + step, outer) * INNER + lane_pos)
+            greet(slabs - 1, row_peer(step))
 
     @pl.when(jnp.logical_not(first_slab))
     def _():
         for step in range(outer):
-            greet(slab - 1, lax.rem(my_outer + step, outer) * INNER + lane_pos)
-
-    peers = jnp.where(first_slab, outer, 1) + jnp.where(last_slab, 0, outer)
+            greet(slab - 1, row_peer(step))
+
+    peers = jnp.where(last_slab, outer, outer + 1)
     pl.semaphore_wait(barrier, peers)
 
     def first_copy(front, step):
-        target = lax.rem(my_outer + step, outer) * INNER + lane_pos
         return pltpu.make_async_remote_copy(
-            src_ref=entering.at[front, me],
+            src_ref=first_out.at[front],
             dst_ref=entering.at[front, me],
-            send_sem=direct_sem.at[1, front, step],
+            send_sem=direct_sem.at[front, step],
             recv_sem=recv_sem.at[front, me],
-            device_id={"slab": slab, "trace": target},
+            device_id={"slab": 0, "trace": row_peer(step)},
             device_id_type=MESH,
         )
 
     def next_copy(front, step):
-        target = lax.rem(my_outer + step, outer) * INNER + lane_pos
         return pltpu.make_async_remote_copy(
             src_ref=leaving.at[front],
             dst_ref=entering.at[front, me],
-            send_sem=direct_sem.at[0, front, step],
+            send_sem=direct_sem.at[front, step],
             recv_sem=recv_sem.at[front, me],
-            device_id={"slab": slab + 1, "trace": target},
+            device_id={"slab": slab + 1, "trace": row_peer(step)},
             device_id_type=MESH,
         )
 
@@ -145,14 +166,20 @@
 
     @pl.when(first_slab)
     def _():
-        load_incident.wait()
         for front in range(fronts):
+            load_incident(front).wait()
             entering[front, me] = incoming[front].astype(jnp.bfloat16)
-        for step in range(1, outer):
-            first_copy(0, step).start()
+
+    @pl.when(last_slab)
+    def _():
+        for front in range(fronts):
+            load_incident(front).wait()
+            first_out[front] = incoming[front].astype(jnp.bfloat16)
+            for step in visit_order(outer)[1:]:
+                first_copy(front, step).start()
 
     def chunk_at(order):
-        return lax.rem(my_chunk + order, chunks)
+        return flip(my_chunk, visit_order(chunks)[order])
 
     def vectors(front, chunk):
         return entering[front, pl.ds(chunk * per_chunk, per_chunk)].reshape(width, columns)
@@ -176,11 +203,6 @@
             store_inner(front).start()
 
     def one_front(front, carry):
-        @pl.when(first_slab & (front + 1 < fronts))
-        def _():
-            for step in range(1, outer):
-                first_copy(front + 1, step).start()
-
         for order in range(chunks):
             for index in range(per_chunk // INNER):
                 block = chunk_at(order) * per_chunk + index * INNER + lane_pos
@@ -213,7 +235,7 @@
 
         @pl.when(jnp.logical_not(last_slab))
         def _():
-            for step in range(outer):
+            for step in visit_order(outer):
                 next_copy(front, step).start()
 
         store_trace(front).start()
@@ -224,7 +246,7 @@
         inner_chunk(fronts - 1, order)
 
     def drain(front, carry):
-        @pl.when(first_slab)
+        @pl.when(last_slab)
         def _():
             for step in range(1, outer):
                 first_copy(front, step).wait_send()
@@ -248,6 +270,7 @@
     inner_rows = green_interior.shape[2]
     depth = green_next.shape[3]
     outer = blocks // INNER
+    in_hbm = pl.BlockSpec(memory_space=pltpu.HBM)
     anywhere = pl.BlockSpec(memory_space=pl.ANY)
     return pl.pallas_call(
         functools.partial(kernel, slabs, blocks),
@@ -255,10 +278,11 @@
             jax.ShapeDtypeStruct((1, fronts, inner_rows, columns), jnp.float32),
             jax.ShapeDtypeStruct((1, fronts, rows, columns), jnp.float32),
         ),
-        in_specs=[anywhere] * 4,
+        in_specs=[in_hbm] * 4,
         out_specs=(anywhere, anywhere),
         scratch_shapes=[
             pltpu.VMEM((fronts, blocks, rows, columns), jnp.bfloat16),
+            pltpu.VMEM((fronts, rows, columns), jnp.bfloat16),
             pltpu.VMEM((fronts, rows, columns), jnp.bfloat16),
             pltpu.VMEM((2, rows, depth), jnp.bfloat16),
             pltpu.VMEM((2, inner_rows, depth), jnp.bfloat16),
@@ -269,9 +293,9 @@
             pltpu.VMEM((fronts, rows, columns), jnp.float32),
             pltpu.VMEM((fronts, inner_rows, columns), jnp.float32),
             pltpu.SemaphoreType.DMA((fronts, blocks)),
-            pltpu.SemaphoreType.DMA((2, fronts, outer)),
             pltpu.SemaphoreType.DMA((fronts, outer)),
-            pltpu.SemaphoreType.DMA((4,)),
+            pltpu.SemaphoreType.DMA((fronts, outer)),
+            pltpu.SemaphoreType.DMA((3 + fronts,)),
             pltpu.SemaphoreType.DMA((2, fronts)),
         ],
         compiler_params=pltpu.CompilerParams(

time: 102 us -> 101 us (level)
  Pallas kernels: 97.4 us -> 95.6 us
    pallas_call x1, Pallas kernels: 97.4 us -> 95.6 us  [local(): pl.pallas_call(functools.partial(kernel, slabs, blocks), out_shape=(jax.S...]
where the time goes in v2:
time: 101 us; the launch traced here: 100 us
  Pallas kernels  95.6 us (95%)
  local copies, waits for them, and re-layouts  4.15 us (4%)
    pallas_call x1, Pallas kernels, local(): pl.pallas_call(functools.partial(kernel, slabs, blocks), out_shape=(jax.S...  95.6 us
    unnamed x6, local copies, waits for them, and re-layouts  4.15 us

profile of v2, /device:TPU:23, one launch (start us, length us, event | category | flops | bytes accessed | tf_op | source)
XLA Modules:
  0.0 100.4 jit_solution(18191277308163574216)
XLA Ops:
  0.6 0.0 copy-start
  0.6 1.1 %copy-done = f32[4,384,128]{2,1,0:T(8,128)S(1)} copy-done((f32[4,384,128]{2,1,0:T(8,128)S(1)}, f32[4,384,128]{2,1,0:T(8,128)}, u32[]{:S(2)}) %copy-start) | copy-done | bytes 786456
  1.8 0.0 copy-start.1
  1.8 1.1 %copy-done.1 = f32[1,4,384,128]{3,2,1,0:T(8,128)S(1)} copy-done((f32[1,4,384,128]{3,2,1,0:T(8,128)S(1)}, f32[1,4,384,128]{3,2,1,0:T(8,128)}, u32[]{:S(2)}) %copy-start.1) | copy-done | bytes 786456
  2.9 95.6 %shard_map.59 = (f32[1,4,576,128]{3,2,1,0:T(8,128)S(1)}, f32[1,4,384,128]{3,2,1,0:T(8,128)S(1)}) custom-call(f32[4,384,128]{2,1,0:T(8,128)S(1)} %copy-done, bf16[1,2,576,3072]{3,2,1,0:T(8,128)(2,1)} %green_interior.1, bf16[1,2,384,3072]{3,2,1,0:T(8,128)(2,1)} %green_next.1, f32[1,4,384,128]{3,2,1,0:T(8,128)S(1)} %copy-done.1), custom_call_target="tpu_custom_call" | custom-call | tf_op jit(solution)/shard_map/pallas_call | solution.py:275
  98.5 1.0 %copy.8 = f32[1,4,576,128]{3,2,1,0:T(8,128)} copy(f32[1,4,576,128]{3,2,1,0:T(8,128)S(1)} %get-tuple-element.4) | data formatting | bytes 2359296
  99.5 0.9 copy.9
Async XLA Ops:
  0.6 1.1 %copy-start = (f32[4,384,128]{2,1,0:T(8,128)S(1)}, f32[4,384,128]{2,1,0:T(8,128)}, u32[]{:S(2)}) copy-start(f32[4,384,128]{2,1,0:T(8,128)} %incident.1) | copy-start | bytes 2359300
  1.8 1.1 %copy-start.1 = (f32[1,4,384,128]{3,2,1,0:T(8,128)S(1)}, f32[1,4,384,128]{3,2,1,0:T(8,128)}, u32[]{:S(2)}) copy-start(f32[1,4,384,128]{3,2,1,0:T(8,128)} %sources.1) | copy-start | bytes 2359300
